TPU v7x, 32 devices: a whole 2x2x4 slice. The times are simulated.
32 devices in a mesh: blk: 8 (over z, x), mp: 4 (over y, core).
Axes of the slice: x: 2, y: 2, z: 4, core: 2. Of those that a mesh axis runs over, the one named last changes fastest.
Arguments:
- lengths: int32 [4], replicated, may hold values from 1 to 512, 1024 in all
- groups: int32 [4], replicated, may hold values from 0 to 3, as said below
- deal: int32 [1024], P('blk'), may hold values from 0 to 1023, as said below
- prefix_block: int32 [8], P('blk'), may hold values from 0 to 7, each once
- queries: bfloat16 [1024, 2048], P('blk', 'mp'), may hold values from -8 to 8
- keys: bfloat16 [1024, 512], P('blk', 'mp'), may hold values from -8 to 8
- values: bfloat16 [1024, 512], P('blk', 'mp'), may hold values from -6 to 6
- prefix_key_blocks: bfloat16 [512, 512], P('blk', 'mp'), may hold values from -8 to 8
- prefix_value_blocks: bfloat16 [512, 512], P('blk', 'mp'), may hold values from -6 to 6
- out_weight: bfloat16 [2048, 4096], P('mp'), may hold values from -0.125 to 0.125
Outputs:
- layer_out: bfloat16 [1024, 4096], P('blk', 'mp')
Inputs may be any that keep to these rules, and one draw needn't show every extreme that they name: The 4 lengths sum to 1024; the largest is 512. `groups`: each group has exactly 1 request. `deal`: a permutation of the request-order rows; on every index of blk, the 16 slots c * 16 to c * 16 + 15 hold rows taken from request-order rows c * 128 to c * 128 + 127, and over all indices of blk each of those rows appears once. `prefix_block`: a permutation of the blocks.
All inputs are finite; a program needn't handle non-finite values.
Results may differ from a plain program's by a relative error of at most 0.012.
Values may be sent and summed in bfloat16 or wider, within the bound.
A program may use at most 64 MiB of HBM per device.

v0:
```python
import math
import jax
import jax.numpy as jnp
from jax import lax
from jax.sharding import PartitionSpec as P

HEAD_WIDTH = 128
GROUPS = 4
NEGATIVE = -1e30


def request_index(row_ids, req_ends):
    return jnp.sum((row_ids[:, None] >= req_ends[None, :]).astype(jnp.int32), axis=1)


def lookup(values_table, indices):
    slots = jnp.arange(values_table.shape[0], dtype=jnp.int32)
    return jnp.sum(jnp.where(indices[:, None] == slots[None, :], values_table[None, :], 0), axis=1)


def attend(flash_state, grouped, key_block, value_block, visible):
    run_best, run_total, run_accum = flash_state
    key_count = key_block.shape[0]
    kv_heads = grouped.shape[1]
    head_size = grouped.shape[3]
    score_scale = 1.0 / math.sqrt(head_size)
    keys_three = key_block.reshape(key_count, kv_heads, head_size)
    values_three = value_block.reshape(key_count, kv_heads, head_size)
    scores = (
        jnp.einsum("rgjd,ngd->rgjn", grouped, keys_three, preferred_element_type=jnp.float32)
        * score_scale
    )
    shown = visible[:, None, None, :]
    scores = jnp.where(shown, scores, NEGATIVE)
    new_best = jnp.maximum(run_best, jnp.max(scores, axis=3))
    weights = jnp.where(shown, jnp.exp(scores - new_best[..., None]), 0.0)
    factor = jnp.exp(run_best - new_best)
    run_total = run_total * factor + jnp.sum(weights, axis=3)
    mixed = jnp.einsum(
        "rgjn,ngd->rgjd",
        weights.astype(jnp.bfloat16),
        values_three,
        preferred_element_type=jnp.float32,
    )
    run_accum = run_accum * factor[..., None] + mixed
    return (new_best, run_total, run_accum)


def sweep(flash_state, grouped, key_block, value_block, key_info, visible_of):
    key_count = key_block.shape[0]
    step_width = key_count if key_count <= 1024 else math.gcd(key_count, 512)
    if step_width == key_count:
        return attend(flash_state, grouped, key_block, value_block, visible_of(key_info))

    def one_step(carried, step_index):
        offset = step_index * step_width
        key_part = lax.dynamic_slice_in_dim(key_block, offset, step_width, 0)
        value_part = lax.dynamic_slice_in_dim(value_block, offset, step_width, 0)
        info_part = lax.dynamic_slice_in_dim(key_info, offset, step_width, 0)
        return (attend(carried, grouped, key_part, value_part, visible_of(info_part)), None)

    flash_state, _ = lax.scan(
        one_step, flash_state, jnp.arange(key_count // step_width, dtype=jnp.int32)
    )
    return flash_state


def shards(
    lengths,
    groups,
    deal,
    prefix_block,
    queries,
    keys,
    values,
    prefix_key_blocks,
    prefix_value_blocks,
    out_weight,
):
    count_rows = queries.shape[0]
    kv_heads = keys.shape[1] // HEAD_WIDTH
    query_per_key_head = queries.shape[1] // keys.shape[1]
    devices = lax.axis_size("blk")
    my_index = lax.axis_index("blk")
    piece_rows = count_rows // devices
    per_group = devices // GROUPS
    prefix_rows = prefix_key_blocks.shape[0]
    req_ends = jnp.cumsum(lengths)
    arrived = lax.all_to_all(
        deal.reshape(devices, piece_rows), "blk", split_axis=0, concat_axis=0, tiled=True
    )
    placed = arrived.reshape(count_rows) - my_index * count_rows

    def prefix_pass(flash_state, grouped, query_group, block_ids):

        def prefix_step(carried, kv_piece):
            key_count = kv_piece[0].shape[0]
            owners = jnp.arange(key_count, dtype=jnp.int32) // prefix_rows
            key_group = jnp.take(block_ids, owners) // per_group

            def same_group(key_info):
                return key_info[None, :] == query_group[:, None]

            return sweep(carried, grouped, kv_piece[0], kv_piece[1], key_group, same_group)

        return prefix_step(
            flash_state,
            (
                lax.all_gather(prefix_key_blocks, "blk", axis=0, tiled=True),
                lax.all_gather(prefix_value_blocks, "blk", axis=0, tiled=True),
            ),
        )

    def suffix_rule(query_rows, query_req):

        def same_request(key_info):
            key_req = request_index(key_info, req_ends)
            return (
                (key_info[None, :] >= 0)
                & (key_req[None, :] == query_req[:, None])
                & (key_info[None, :] <= query_rows[:, None])
            )

        return same_request

    key_rows, block_ids = (
        lax.all_gather(deal, "blk", axis=0, tiled=True),
        lax.all_gather(prefix_block, "blk", axis=0, tiled=True),
    )
    query_rows = deal
    query_req = request_index(query_rows, req_ends)
    query_group = lookup(groups, query_req)
    grouped = queries.reshape(count_rows, kv_heads, query_per_key_head, HEAD_WIDTH)
    flash_state = prefix_pass(
        (
            jnp.full((count_rows, kv_heads, query_per_key_head), NEGATIVE, jnp.float32),
            jnp.zeros((count_rows, kv_heads, query_per_key_head), jnp.float32),
            jnp.zeros((count_rows, kv_heads, query_per_key_head, HEAD_WIDTH), jnp.float32),
        ),
        grouped,
        query_group,
        block_ids,
    )
    visible_of = suffix_rule(query_rows, query_req)
    kv_piece = (
        lax.all_gather(keys, "blk", axis=0, tiled=True),
        lax.all_gather(values, "blk", axis=0, tiled=True),
    )
    key_info = key_rows
    flash_state = sweep(flash_state, grouped, kv_piece[0], kv_piece[1], key_info, visible_of)
    run_best, run_total, run_accum = flash_state
    attended = (run_accum / run_total[..., None]).astype(jnp.bfloat16).reshape(count_rows, -1)
    returned = lax.all_to_all(
        attended.reshape(devices, piece_rows, -1), "blk", split_axis=0, concat_axis=0, tiled=True
    )
    flat = returned.reshape(count_rows, returned.shape[2])
    ordered = jnp.zeros_like(flat).at[placed].set(flat)
    partial_value = jnp.dot(ordered, out_weight, preferred_element_type=jnp.float32)
    return lax.psum_scatter(
        partial_value.astype(jnp.bfloat16), "mp", scatter_dimension=1, tiled=True
    )


def solution(mesh):
    return jax.shard_map(
        shards,
        mesh=mesh,
        in_specs=(
            P(),
            P(),
            P("blk"),
            P("blk"),
            P("blk", "mp"),
            P("blk", "mp"),
            P("blk", "mp"),
            P("blk", "mp"),
            P("blk", "mp"),
            P("mp", None),
        ),
        out_specs=P("blk", "mp"),
        check_vma=False,
    )
```

profile of v0, /device:TPU:0, one launch (start us, length us, event | category | flops | bytes accessed | tf_op | source)
XLA Modules:
  0.0 230.1 jit_solution(1636237273558272072)
XLA Ops:
  6.5 1.4 all_to_all.9
  7.9 7.3 %all-to-all-start = ((s32[8,1,16]{2,1,0:T(1,128)}), s32[8,1,16]{2,1,0:T(1,128)S(1)}, u32[]{:S(2)}, u32[]{:S(2)}) async-start(s32[8,1,16]{2,1,0:T(1,128)} %bitcast), calls=%async_computation | async-start | bytes 8192 | tf_op jit(solution)/shard_map/all_to_all | solution.py:89
  15.2 0.8 reduce-window.8
  16.0 0.7 convert_reduce_fusion.1
  16.7 21.0 %all-gather = s32[8,1,128]{2,1,0:T(1,128)S(1)} all-gather(s32[1,1,128]{2,1,0:T(1,128)} %bitcast.108), channel_id=1, replica_groups=mesh['blk'=8,'mp'=4] {'blk'}, dimensions={0}, use_global_device_ids=true | all-gather | bytes 4608 | tf_op jit(solution)/shard_map/all_gather | solution.py:127
  37.7 0.1 convert_reduce_fusion
  38.5 1.2 dynamic-slice
  39.7 0.8 dynamic-update-slice
  40.5 6.8 %all-reduce = s32[8]{0:T(128)S(1)} all-reduce(s32[8]{0:T(128)S(1)} %dynamic-update-slice), channel_id=1, replica_groups=mesh['blk'=8,'mp'=4] {'blk'}, use_global_device_ids=true, to_apply=%add | all-reduce | flops 8 | bytes 64
  47.3 0.7 fusion.47
  48.0 32.5 %all_gather.19 = bf16[512,128]{1,0:T(8,128)(2,1)S(1)} all-gather(bf16[64,128]{1,0:T(8,128)(2,1)} %param.17), channel_id=1, replica_groups=mesh['blk'=8,'mp'=4] {'blk'}, dimensions={0}, use_global_device_ids=true | all-gather | bytes 147456 | tf_op jit(solution)/shard_map/all_gather | solution.py:109
  80.5 30.9 %all_gather.22 = bf16[1024,128]{1,0:T(8,128)(2,1)S(1)} all-gather(bf16[128,128]{1,0:T(8,128)(2,1)} %param.15), channel_id=1, replica_groups=mesh['blk'=8,'mp'=4] {'blk'}, dimensions={0}, use_global_device_ids=true | all-gather | bytes 294912 | tf_op jit(solution)/shard_map/all_gather | solution.py:146
  111.5 31.0 %all_gather.23 = bf16[1024,128]{1,0:T(8,128)(2,1)S(1)} all-gather(bf16[128,128]{1,0:T(8,128)(2,1)} %param.16), channel_id=1, replica_groups=mesh['blk'=8,'mp'=4] {'blk'}, dimensions={0}, use_global_device_ids=true | all-gather | bytes 294912 | tf_op jit(solution)/shard_map/all_gather | solution.py:147
  142.5 0.7 select_reduce_fusion
  143.2 4.3 %compare_select_fusion.1 = s32[512,1]{0,1:T(1,128)S(1)} fusion(s32[]{:T(128)} %bitcast.4, s32[]{:T(128)} %bitcast.5, s32[]{:T(128)} %bitcast.6, s32[]{:T(128)} %bitcast.7, s32[]{:T(128)} %bitcast.8, s32[]{:T(128)} %bitcast.10, s32[]{:T(128)} %bitcast.9), kind=kLoop, calls=%fused_computation.47 | loop fusion | flops 11776 | bytes 2076 | tf_op jit(solution)/shard_map/jit(_take)/gather | solution.py:99
  147.6 0.7 add_select_fusion
  148.2 0.1 broadcast_compare_fusion
  148.4 1.5 compare_and_fusion
  149.9 0.3 fusion.48
  150.2 0.5 fusion
  150.7 0.5 fusion.1
  151.3 0.8 convolution_bitcast_fusion.1
  152.0 30.5 %all_gather.20 = bf16[512,128]{1,0:T(8,128)(2,1)S(1)} all-gather(bf16[64,128]{1,0:T(8,128)(2,1)S(1)} %copy-done.1), channel_id=1, replica_groups=mesh['blk'=8,'mp'=4] {'blk'}, dimensions={0}, use_global_device_ids=true | all-gather | bytes 147456 | tf_op jit(solution)/shard_map/all_gather | solution.py:110
  182.5 0.2 fusion.18
  182.8 0.5 fusion.10
  183.2 0.1 copy.31
  183.4 0.7 reshape_reshape.3
  184.1 4.0 %all-to-all-start.1 = ((bf16[8,16,512]{2,1,0:T(8,128)(2,1)}), bf16[8,16,512]{2,1,0:T(8,128)(2,1)S(1)}, u32[]{:S(2)}, u32[]{:S(2)}) async-start(bf16[8,16,512]{2,1,0:T(8,128)(2,1)} %reshape_reshape.3), calls=%async_computation.1 | async-start | bytes 262144 | tf_op jit(solution)/shard_map/all_to_all | solution.py:153
  188.2 7.2 %all-to-all-done.1 = bf16[8,16,512]{2,1,0:T(8,128)(2,1)S(1)} async-done(((bf16[8,16,512]{2,1,0:T(8,128)(2,1)}), bf16[8,16,512]{2,1,0:T(8,128)(2,1)S(1)}, u32[]{:S(2)}, u32[]{:S(2)}) %all-to-all-start.1) | async-done | bytes 131104 | tf_op jit(solution)/shard_map/all_to_all | solution.py:153
  195.4 1.1 scatter_custom_fusion
  196.5 3.9 %convolution_convert_fusion = bf16[128,4096]{1,0:T(8,128)(2,1)} fusion(bf16[128,512]{1,0:T(8,128)(2,1)S(1)} %scatter_custom_fusion, bf16[512,4096]{1,0:T(8,128)(2,1)} %param.19), kind=kOutput, calls=%fused_computation.1 | convolution fusion | flops 537395200 | bytes 5373952 | tf_op jit(solution)/shard_map/dot_general | solution.py:158
  200.4 22.9 %reduce-scatter.2.cloned.1.call-done = bf16[128,1024]{1,0:T(8,128)(2,1)} async-done(((bf16[128,4096]{1,0:T(8,128)(2,1)}), bf16[128,1024]{1,0:T(8,128)(2,1)}) %reduce-scatter.2.cloned.1.call-update) | async-done | bytes 262160 | tf_op jit(solution)/shard_map/reduce_scatter | solution.py:159
  (15 shorter events, 0.2 us)
Async XLA Ops:
  6.5 143.4 %copy-start = (bf16[128,512]{1,0:T(8,128)(2,1)S(1)}, bf16[128,512]{1,0:T(8,128)(2,1)}, u32[]{:S(2)}) copy-start(bf16[128,512]{1,0:T(8,128)(2,1)} %param.14) | copy-start | bytes 393220
  7.9 176.2 %all-to-all-start = ((s32[8,1,16]{2,1,0:T(1,128)}), s32[8,1,16]{2,1,0:T(1,128)S(1)}, u32[]{:S(2)}, u32[]{:S(2)}) async-start(s32[8,1,16]{2,1,0:T(1,128)} %bitcast), calls=%async_computation | async-start | bytes 8192 | tf_op jit(solution)/shard_map/all_to_all | solution.py:89
  151.2 0.8 copy-start.1
  184.1 11.3 %all-to-all-start.1 = ((bf16[8,16,512]{2,1,0:T(8,128)(2,1)}), bf16[8,16,512]{2,1,0:T(8,128)(2,1)S(1)}, u32[]{:S(2)}, u32[]{:S(2)}) async-start(bf16[8,16,512]{2,1,0:T(8,128)(2,1)} %reshape_reshape.3), calls=%async_computation.1 | async-start | bytes 262144 | tf_op jit(solution)/shard_map/all_to_all | solution.py:153
  188.1 35.2 %reduce-scatter.2.cloned.1.call-start = ((), (), s32[]{:S(2)}) async-start(), calls=%async_computation.3 | async-start | bytes 1310720 | tf_op jit(solution)/shard_map/reduce_scatter | solution.py:159
Sparse Core Ops, SparseCore 0:
  200.5 22.6 reduce-scatter.1
where the time goes:
time: 231 us; the launch traced here: 230 us
  blocking collectives  153 us (66%)
  waiting for transfers between devices  30.1 us (13%)
  between operations  14.2 us (6%)
  starting transfers between devices  11.3 us (5%)
  other arithmetic  9.85 us (4%)
  local copies, waits for them, and re-layouts  6.03 us (3%)
  matrix products  5.89 us (3%)
    all_gather x1, blocking collectives, prefix_pass(): lax.all_gather(prefix_key_blocks, 'blk', axis=0, tiled=True)  32.5 us
    all_gather x1, blocking collectives, shards(): lax.all_gather(values, 'blk', axis=0, tiled=True)  31 us
    all_gather x1, blocking collectives, shards(): lax.all_gather(keys, 'blk', axis=0, tiled=True)  30.9 us
    all_gather x1, blocking collectives, prefix_pass(): lax.all_gather(prefix_value_blocks, 'blk', axis=0, tiled=True)  30.5 us
    reduce_scatter x1, waiting for transfers between devices, shards(): lax.psum_scatter(partial_value.astype(jnp.bfloat16), 'mp', scatter_dimens...  22.9 us
    all_gather x1, blocking collectives, shards(): lax.all_gather(deal, 'blk', axis=0, tiled=True)  21 us
    all_to_all x1, starting transfers between devices, shards(): lax.all_to_all(deal.reshape(devices, piece_rows), 'blk', split_axis=0, co...  7.25 us
    all_to_all x1, waiting for transfers between devices, shards(): lax.all_to_all(attended.reshape(devices, piece_rows, -1), 'blk', split_ax...  7.19 us
  transfers between devices with their start and end apart: 3, of which 2 were waited for; matrix products, arithmetic and copies ran while one was open for 7% of the time, Pallas kernels for 0%

commit v1 on v0

--- a/solution.py
+++ b/solution.py
@@ -7,6 +7,27 @@
 HEAD_WIDTH = 128
 GROUPS = 4
 NEGATIVE = -1e30
+
+
+def collect(x, axis, dim):
+    devices, position, width = (lax.axis_size(axis), lax.axis_index(axis), x.shape[dim])
+    forward = [(i, (i + 1) % devices) for i in range(devices)]
+    behind = [(i, (i - 1) % devices) for i in range(devices)]
+    filled = jnp.zeros((*x.shape[:dim], devices * width, *x.shape[dim + 1 :]), x.dtype)
+    filled = lax.dynamic_update_slice_in_dim(filled, x, position * width, axis=dim)
+    from_left = from_right = x
+    middle = devices // 2
+    for lap in range(1, middle + 1):
+        from_left = lax.ppermute(from_left, axis, forward)
+        filled = lax.dynamic_update_slice_in_dim(
+            filled, from_left, (position - lap) % devices * width, axis=dim
+        )
+        if lap < devices - middle:
+            from_right = lax.ppermute(from_right, axis, behind)
+            filled = lax.dynamic_update_slice_in_dim(
+                filled, from_right, (position + lap) % devices * width, axis=dim
+            )
+    return filled
 
 
 def request_index(row_ids, req_ends):
@@ -106,7 +127,7 @@
         return prefix_step(
             flash_state,
             (
-                lax.all_gather(prefix_key_blocks, "blk", axis=0, tiled=True),
+                collect(prefix_key_blocks, "blk", 0),
                 lax.all_gather(prefix_value_blocks, "blk", axis=0, tiled=True),
             ),
         )

time: 231 us -> 222 us (0.961)
  blocking collectives: 153 us -> 122 us
  starting transfers between devices: 11.3 us -> 22.2 us
  waiting for transfers between devices: 30.1 us -> 39.9 us
    all_gather x1 -> x0, blocking collectives: 32.5 us -> none  [prefix_pass(): lax.all_gather(prefix_key_blocks, 'blk', axis=0, tiled=True)]
    ppermute x0 -> x7, starting transfers between devices: none -> 15.4 us  [the longest x3 12.5 us: collect(): from_right = lax.ppermute(from_right, axis, behind)]
    ppermute x0 -> x7, waiting for transfers between devices: none -> 9.8 us  [the longest x4 9.79 us: collect(): from_left = lax.ppermute(from_left, axis, forward)]
    all_to_all x1, starting transfers between devices: 7.25 us -> 3.33 us  [shards(): lax.all_to_all(deal.reshape(devices, piece_rows), 'blk', split_axis=0, co...]
  transfers between devices with their start and end apart: 3 -> 10, of which waited for: 2 -> 5; matrix products, arithmetic and copies ran while one was open for 7% -> 7% of each run, Pallas kernels for 0% -> 0%
where the time goes in v1:
time: 222 us; the launch traced here: 221 us
  blocking collectives  122 us (55%)
  waiting for transfers between devices  39.9 us (18%)
  starting transfers between devices  22.2 us (10%)
  between operations  14.2 us (6%)
  other arithmetic  9.86 us (4%)
  local copies, waits for them, and re-layouts  6.81 us (3%)
  matrix products  5.88 us (3%)
    all_gather x1, blocking collectives, shards(): lax.all_gather(keys, 'blk', axis=0, tiled=True)  32.7 us
    all_gather x1, blocking collectives, shards(): lax.all_gather(values, 'blk', axis=0, tiled=True)  31 us
    all_gather x1, blocking collectives, prefix_pass(): lax.all_gather(prefix_value_blocks, 'blk', axis=0, tiled=True)  30.8 us
    reduce_scatter x1, waiting for transfers between devices, shards(): lax.psum_scatter(partial_value.astype(jnp.bfloat16), 'mp', scatter_dimens...  22.9 us
    all_gather x1, blocking collectives, shards(): lax.all_gather(deal, 'blk', axis=0, tiled=True)  21 us
    ppermute x3, starting transfers between devices, collect(): from_right = lax.ppermute(from_right, axis, behind)  12.5 us
    ppermute x4, waiting for transfers between devices, collect(): from_left = lax.ppermute(from_left, axis, forward)  9.79 us
    all_to_all x1, waiting for transfers between devices, shards(): lax.all_to_all(attended.reshape(devices, piece_rows, -1), 'blk', split_ax...  7.12 us
  transfers between devices with their start and end apart: 10, of which 5 were waited for; matrix products, arithmetic and copies ran while one was open for 7% of the time, Pallas kernels for 0%

profile of v1, /device:TPU:0, one launch (start us, length us, event | category | flops | bytes accessed | tf_op | source)
XLA Modules:
  0.0 221.1 jit_solution(3949350005986247833)
XLA Ops:
  6.5 2.9 %collective-permute-start = (bf16[64,128]{1,0:T(8,128)(2,1)}, bf16[64,128]{1,0:T(8,128)(2,1)S(1)}, u32[]{:S(2)}, u32[]{:S(2)}) collective-permute-start(bf16[64,128]{1,0:T(8,128)(2,1)} %param.17), channel_id=1, source_target_pairs={{0,4},{4,8},{8,12},{12,16},{16,20},{20,24},{24,28},{28,0},{1,5},{5... | collective-permute-start | bytes 49160 | tf_op jit(solution)/shard_map/ppermute | solution.py:21
  9.5 3.0 %collective-permute-start.1 = (bf16[64,128]{1,0:T(8,128)(2,1)}, bf16[64,128]{1,0:T(8,128)(2,1)S(1)}, u32[]{:S(2)}, u32[]{:S(2)}) collective-permute-start(bf16[64,128]{1,0:T(8,128)(2,1)} %param.17), channel_id=1, source_target_pairs={{0,28},{4,0},{8,4},{12,8},{16,12},{20,16},{24,20},{28,24},{1,29},{... | collective-permute-start | bytes 49160 | tf_op jit(solution)/shard_map/ppermute | solution.py:26
  12.5 1.3 all_to_all.9
  13.8 3.3 %all-to-all-start = ((s32[8,1,16]{2,1,0:T(1,128)}), s32[8,1,16]{2,1,0:T(1,128)S(1)}, u32[]{:S(2)}, u32[]{:S(2)}) async-start(s32[8,1,16]{2,1,0:T(1,128)} %bitcast), calls=%async_computation | async-start | bytes 8192 | tf_op jit(solution)/shard_map/all_to_all | solution.py:110
  17.2 0.8 reduce-window.8
  18.1 0.7 convert_reduce_fusion.1
  18.8 21.0 %all-gather = s32[8,1,128]{2,1,0:T(1,128)S(1)} all-gather(s32[1,1,128]{2,1,0:T(1,128)} %bitcast.108), channel_id=1, replica_groups=mesh['blk'=8,'mp'=4] {'blk'}, dimensions={0}, use_global_device_ids=true | all-gather | bytes 4608 | tf_op jit(solution)/shard_map/all_gather | solution.py:148
  40.5 1.2 dynamic-slice
  41.8 0.8 dynamic-update-slice
  42.5 6.8 %all-reduce = s32[8]{0:T(128)S(1)} all-reduce(s32[8]{0:T(128)S(1)} %dynamic-update-slice), channel_id=1, replica_groups=mesh['blk'=8,'mp'=4] {'blk'}, use_global_device_ids=true, to_apply=%add | all-reduce | flops 8 | bytes 64
  49.3 0.7 fusion.47
  50.0 32.7 %all_gather.18 = bf16[1024,128]{1,0:T(8,128)(2,1)S(1)} all-gather(bf16[128,128]{1,0:T(8,128)(2,1)} %param.15), channel_id=1, replica_groups=mesh['blk'=8,'mp'=4] {'blk'}, dimensions={0}, use_global_device_ids=true | all-gather | bytes 294912 | tf_op jit(solution)/shard_map/all_gather | solution.py:167
  82.7 31.0 %all_gather.19 = bf16[1024,128]{1,0:T(8,128)(2,1)S(1)} all-gather(bf16[128,128]{1,0:T(8,128)(2,1)} %param.16), channel_id=1, replica_groups=mesh['blk'=8,'mp'=4] {'blk'}, dimensions={0}, use_global_device_ids=true | all-gather | bytes 294912 | tf_op jit(solution)/shard_map/all_gather | solution.py:168
  113.8 0.7 constant_dynamic-update-slice_fusion.7
  114.5 0.7 select_reduce_fusion
  115.2 4.3 %compare_select_fusion.1 = s32[512,1]{0,1:T(1,128)S(1)} fusion(s32[]{:T(128)} %bitcast.4, s32[]{:T(128)} %bitcast.5, s32[]{:T(128)} %bitcast.6, s32[]{:T(128)} %bitcast.7, s32[]{:T(128)} %bitcast.8, s32[]{:T(128)} %bitcast.10, s32[]{:T(128)} %bitcast.9), kind=kLoop, calls=%fused_computation.47 | loop fusion | flops 11776 | bytes 2076 | tf_op jit(solution)/shard_map/jit(_take)/gather | solution.py:120
  119.5 0.7 add_select_fusion
  120.3 1.5 compare_and_fusion
  122.4 30.8 %all_gather.16 = bf16[512,128]{1,0:T(8,128)(2,1)S(1)} all-gather(bf16[64,128]{1,0:T(8,128)(2,1)S(1)} %copy-done.1), channel_id=1, replica_groups=mesh['blk'=8,'mp'=4] {'blk'}, dimensions={0}, use_global_device_ids=true | all-gather | bytes 147456 | tf_op jit(solution)/shard_map/all_gather | solution.py:131
  153.2 4.7 %collective-permute-start.3 = (bf16[64,128]{1,0:T(8,128)(2,1)S(1)}, bf16[64,128]{1,0:T(8,128)(2,1)S(1)}, u32[]{:S(2)}, u32[]{:S(2)}) collective-permute-start(bf16[64,128]{1,0:T(8,128)(2,1)S(1)} %collective-permute-done.1), channel_id=1, source_target_pairs={{0,28},{4,0},{8,4},{12,8},{16,12},{20,16},{24,20},{28,24},{1,29},{... | collective-permute-start | bytes 49160 | tf_op jit(solution)/shard_map/ppermute | solution.py:26
  157.9 1.7 collective-permute-done.2
  159.6 4.7 %collective-permute-start.5 = (bf16[64,128]{1,0:T(8,128)(2,1)S(1)}, bf16[64,128]{1,0:T(8,128)(2,1)S(1)}, u32[]{:S(2)}, u32[]{:S(2)}) collective-permute-start(bf16[64,128]{1,0:T(8,128)(2,1)S(1)} %collective-permute-done.3), channel_id=1, source_target_pairs={{0,28},{4,0},{8,4},{12,8},{16,12},{20,16},{24,20},{28,24},{1,29},{... | collective-permute-start | bytes 49160 | tf_op jit(solution)/shard_map/ppermute | solution.py:26
  164.3 1.7 collective-permute-done.4
  166.1 6.4 %collective-permute-done.6 = bf16[64,128]{1,0:T(8,128)(2,1)S(1)} collective-permute-done((bf16[64,128]{1,0:T(8,128)(2,1)S(1)}, bf16[64,128]{1,0:T(8,128)(2,1)S(1)}, u32[]{:S(2)}, u32[]{:S(2)}) %collective-permute-start.6) | collective-permute-done | bytes 16416 | tf_op jit(solution)/shard_map/ppermute | solution.py:21
  172.8 0.5 fusion.1
  173.3 0.7 convolution_bitcast_fusion.1
  174.9 0.7 reshape_reshape.3
  175.6 3.4 %all-to-all-start.1 = ((bf16[8,16,512]{2,1,0:T(8,128)(2,1)}), bf16[8,16,512]{2,1,0:T(8,128)(2,1)S(1)}, u32[]{:S(2)}, u32[]{:S(2)}) async-start(bf16[8,16,512]{2,1,0:T(8,128)(2,1)} %reshape_reshape.3), calls=%async_computation.1 | async-start | bytes 262144 | tf_op jit(solution)/shard_map/all_to_all | solution.py:174
  179.2 7.1 %all-to-all-done.1 = bf16[8,16,512]{2,1,0:T(8,128)(2,1)S(1)} async-done(((bf16[8,16,512]{2,1,0:T(8,128)(2,1)}), bf16[8,16,512]{2,1,0:T(8,128)(2,1)S(1)}, u32[]{:S(2)}, u32[]{:S(2)}) %all-to-all-start.1) | async-done | bytes 131104 | tf_op jit(solution)/shard_map/all_to_all | solution.py:174
  186.3 1.1 scatter_custom_fusion
  187.4 3.9 %convolution_convert_fusion = bf16[128,4096]{1,0:T(8,128)(2,1)} fusion(bf16[128,512]{1,0:T(8,128)(2,1)S(1)} %scatter_custom_fusion, bf16[512,4096]{1,0:T(8,128)(2,1)} %param.19), kind=kOutput, calls=%fused_computation.1 | convolution fusion | flops 537395200 | bytes 5373952 | tf_op jit(solution)/shard_map/dot_general | solution.py:179
  191.3 22.9 %reduce-scatter.2.cloned.1.call-done = bf16[128,1024]{1,0:T(8,128)(2,1)} async-done(((bf16[128,4096]{1,0:T(8,128)(2,1)}), bf16[128,1024]{1,0:T(8,128)(2,1)}) %reduce-scatter.2.cloned.1.call-update) | async-done | bytes 262160 | tf_op jit(solution)/shard_map/reduce_scatter | solution.py:180
  (37 shorter events, 2.1 us)
Async XLA Ops:
  6.5 115.4 %copy-start = (bf16[128,512]{1,0:T(8,128)(2,1)S(1)}, bf16[128,512]{1,0:T(8,128)(2,1)}, u32[]{:S(2)}) copy-start(bf16[128,512]{1,0:T(8,128)(2,1)} %param.14) | copy-start | bytes 393220
  6.5 115.8 %copy-start.1 = (bf16[64,128]{1,0:T(8,128)(2,1)S(1)}, bf16[64,128]{1,0:T(8,128)(2,1)}, u32[]{:S(2)}) copy-start(bf16[64,128]{1,0:T(8,128)(2,1)} %param.18) | copy-start | bytes 49156
  6.5 146.6 %collective-permute-start = (bf16[64,128]{1,0:T(8,128)(2,1)}, bf16[64,128]{1,0:T(8,128)(2,1)S(1)}, u32[]{:S(2)}, u32[]{:S(2)}) collective-permute-start(bf16[64,128]{1,0:T(8,128)(2,1)} %param.17), channel_id=1, source_target_pairs={{0,4},{4,8},{8,12},{12,16},{16,20},{20,24},{24,28},{28,0},{1,5},{5... | collective-permute-start | bytes 49160 | tf_op jit(solution)/shard_map/ppermute | solution.py:21
  9.5 143.7 %collective-permute-start.1 = (bf16[64,128]{1,0:T(8,128)(2,1)}, bf16[64,128]{1,0:T(8,128)(2,1)S(1)}, u32[]{:S(2)}, u32[]{:S(2)}) collective-permute-start(bf16[64,128]{1,0:T(8,128)(2,1)} %param.17), channel_id=1, source_target_pairs={{0,28},{4,0},{8,4},{12,8},{16,12},{20,16},{24,20},{28,24},{1,29},{... | collective-permute-start | bytes 49160 | tf_op jit(solution)/shard_map/ppermute | solution.py:26
  13.8 161.8 %all-to-all-start = ((s32[8,1,16]{2,1,0:T(1,128)}), s32[8,1,16]{2,1,0:T(1,128)S(1)}, u32[]{:S(2)}, u32[]{:S(2)}) async-start(s32[8,1,16]{2,1,0:T(1,128)} %bitcast), calls=%async_computation | async-start | bytes 8192 | tf_op jit(solution)/shard_map/all_to_all | solution.py:110
  153.1 6.5 %collective-permute-start.2 = (bf16[64,128]{1,0:T(8,128)(2,1)S(1)}, bf16[64,128]{1,0:T(8,128)(2,1)S(1)}, u32[]{:S(2)}, u32[]{:S(2)}) collective-permute-start(bf16[64,128]{1,0:T(8,128)(2,1)S(1)} %collective-permute-done), channel_id=1, source_target_pairs={{0,4},{4,8},{8,12},{12,16},{16,20},{20,24},{24,28},{28,0},{1,5},{5... | collective-permute-start | bytes 49160 | tf_op jit(solution)/shard_map/ppermute | solution.py:21
  153.2 6.4 %collective-permute-start.3 = (bf16[64,128]{1,0:T(8,128)(2,1)S(1)}, bf16[64,128]{1,0:T(8,128)(2,1)S(1)}, u32[]{:S(2)}, u32[]{:S(2)}) collective-permute-start(bf16[64,128]{1,0:T(8,128)(2,1)S(1)} %collective-permute-done.1), channel_id=1, source_target_pairs={{0,28},{4,0},{8,4},{12,8},{16,12},{20,16},{24,20},{28,24},{1,29},{... | collective-permute-start | bytes 49160 | tf_op jit(solution)/shard_map/ppermute | solution.py:26
  159.6 6.4 %collective-permute-start.4 = (bf16[64,128]{1,0:T(8,128)(2,1)S(1)}, bf16[64,128]{1,0:T(8,128)(2,1)S(1)}, u32[]{:S(2)}, u32[]{:S(2)}) collective-permute-start(bf16[64,128]{1,0:T(8,128)(2,1)S(1)} %collective-permute-done.2), channel_id=1, source_target_pairs={{0,4},{4,8},{8,12},{12,16},{16,20},{20,24},{24,28},{28,0},{1,5},{5... | collective-permute-start | bytes 49160 | tf_op jit(solution)/shard_map/ppermute | solution.py:21
  159.6 6.4 %collective-permute-start.5 = (bf16[64,128]{1,0:T(8,128)(2,1)S(1)}, bf16[64,128]{1,0:T(8,128)(2,1)S(1)}, u32[]{:S(2)}, u32[]{:S(2)}) collective-permute-start(bf16[64,128]{1,0:T(8,128)(2,1)S(1)} %collective-permute-done.3), channel_id=1, source_target_pairs={{0,28},{4,0},{8,4},{12,8},{16,12},{20,16},{24,20},{28,24},{1,29},{... | collective-permute-start | bytes 49160 | tf_op jit(solution)/shard_map/ppermute | solution.py:26
  166.0 6.4 %collective-permute-start.6 = (bf16[64,128]{1,0:T(8,128)(2,1)S(1)}, bf16[64,128]{1,0:T(8,128)(2,1)S(1)}, u32[]{:S(2)}, u32[]{:S(2)}) collective-permute-start(bf16[64,128]{1,0:T(8,128)(2,1)S(1)} %collective-permute-done.4), channel_id=1, source_target_pairs={{0,4},{4,8},{8,12},{12,16},{16,20},{20,24},{24,28},{28,0},{1,5},{5... | collective-permute-start | bytes 49160 | tf_op jit(solution)/shard_map/ppermute | solution.py:21
  175.6 10.7 %all-to-all-start.1 = ((bf16[8,16,512]{2,1,0:T(8,128)(2,1)}), bf16[8,16,512]{2,1,0:T(8,128)(2,1)S(1)}, u32[]{:S(2)}, u32[]{:S(2)}) async-start(bf16[8,16,512]{2,1,0:T(8,128)(2,1)} %reshape_reshape.3), calls=%async_computation.1 | async-start | bytes 262144 | tf_op jit(solution)/shard_map/all_to_all | solution.py:174
  179.0 35.2 %reduce-scatter.2.cloned.1.call-start = ((), (), s32[]{:S(2)}) async-start(), calls=%async_computation.3 | async-start | bytes 1310720 | tf_op jit(solution)/shard_map/reduce_scatter | solution.py:180
Sparse Core Ops, SparseCore 0:
  191.4 22.7 reduce-scatter.1
